TPU v7x, 256 devices: a whole 4x4x8 slice. The times are simulated.
256 devices in a mesh: pipe: 8 (over x, z_hi), expert: 32 (over y, z_lo, core).
Axes of the slice: x: 4, y: 4, z: 8 (z_hi: 2, z_lo: 4; z = z_hi * 4 + z_lo), core: 2. Of those that a mesh axis runs over, the one named last changes fastest.
Arguments:
- fwd_acts: bfloat16 [8, 2048, 3584], P('pipe', 'expert'), may hold values from -6 to 6
- fwd_routes: int32 [8, 2048, 2], P('pipe', 'expert'), may hold values from 0 to 7, all different within a row; in each aligned block of 64 rows (0 to 63, 64 to 127, ..., all dimensions but the last counted through in order) at most 20 rows name the same one
- fwd_gates: float32 [8, 2048, 2], P('pipe', 'expert'), may hold values from 0.25 to 1
- back_acts: bfloat16 [8, 2048, 3584], P('pipe', 'expert'), may hold values from -6 to 6
- back_routes: int32 [8, 2048, 2], P('pipe', 'expert'), may hold values from 0 to 7, all different within a row; in each aligned block of 64 rows (0 to 63, 64 to 127, ..., all dimensions but the last counted through in order) at most 20 rows name the same one
- back_gates: float32 [8, 2048, 2], P('pipe', 'expert'), may hold values from 0.25 to 1
- back_grads: bfloat16 [8, 2048, 3584], P('pipe', 'expert'), may hold values from -0.59765625 to 0.59765625
- w_up: bfloat16 [8, 32, 3584, 256], P('pipe', 'expert'), may hold values from -0.09375 to 0.09375
- w_down: bfloat16 [8, 32, 256, 3584], P('pipe', 'expert'), may hold values from -0.1875 to 0.1875
Outputs:
- fwd_next: bfloat16 [8, 2048, 3584], P('pipe', 'expert')
- back_next: bfloat16 [8, 2048, 3584], P('pipe', 'expert')
- grad_up: float32 [8, 32, 3584, 256], P('pipe', 'expert')
- grad_down: float32 [8, 32, 256, 3584], P('pipe', 'expert')
Inputs may be any that keep to these rules, and one draw needn't show every extreme that they name: `fwd_routes`: in each aligned block of 64 rows of a section the 2 experts of a row differ, and each expert is named by at most 20 rows, by exactly 20 in some block. `back_routes`: as for fwd_routes.
All inputs are finite; a program needn't handle non-finite values.
Results may differ from a plain program's by a relative error of at most 0.005.
Values may be sent and summed in bfloat16 or wider, within the bound.
A program may use at most 192 MiB of HBM per device.

v0:
```python
import jax
import jax.numpy as jnp
from jax import lax
from jax.sharding import PartitionSpec as P

GROUP = 4
HIGH = lax.Precision.HIGHEST


def passed_along(value, axis, steps):
    count = lax.axis_size(axis)
    pairs = [(source, (source + steps) % count) for source in range(count)]
    return lax.ppermute(value, axis, pairs)


def silu_grad(value):
    sigma = jax.nn.sigmoid(value)
    return sigma * (1.0 + value * (1.0 - sigma))


def tables(routes, gates, experts, slot_cap):
    tok_rows, top_count = routes.shape
    flat = routes.reshape(tok_rows * top_count)
    onehot = (flat[:, None] == jnp.arange(experts, dtype=jnp.int32)[None, :]).astype(jnp.int32)
    before = jnp.cumsum(onehot, axis=0) - onehot
    slots = jnp.sum(before * onehot, axis=1)
    places = flat * slot_cap + slots
    columns = jnp.arange(experts * slot_cap, dtype=jnp.int32)
    hits = (
        (places[:, None] == columns[None, :])
        .astype(jnp.float32)
        .reshape(tok_rows, top_count, experts * slot_cap)
    )
    plain = jnp.sum(hits, axis=1)
    gated = jnp.sum(hits * gates[:, :, None], axis=1)
    return (plain, gated)


def gather_rows(plain, values):
    return lax.dot_general(
        plain.astype(jnp.bfloat16),
        values,
        (((0,), (0,)), ((), ())),
        preferred_element_type=jnp.float32,
    ).astype(jnp.bfloat16)


def send_rows(stacked, experts, slot_cap):
    count, _, model_width = stacked.shape
    copies = jnp.repeat(stacked.reshape(count, experts, 1, slot_cap, model_width), GROUP, axis=2)
    copies = copies.reshape(count, experts * GROUP, slot_cap, model_width)
    received = lax.all_to_all(copies, "expert", split_axis=1, concat_axis=1, tiled=True)
    return received.reshape(count, -1, model_width)


def send_back(parts, experts, slot_cap):
    count, _, model_width = parts.shape
    arranged = parts.reshape(count, experts * GROUP, slot_cap, model_width)
    received = lax.all_to_all(arranged, "expert", split_axis=1, concat_axis=1, tiled=True)
    summed = jnp.sum(
        received.reshape(count, experts, GROUP, slot_cap, model_width), axis=2, dtype=jnp.float32
    )
    return summed.reshape(count, experts * slot_cap, model_width)


def expert_forward(rows, up_proj, down_proj):
    pre = jnp.dot(rows, up_proj, preferred_element_type=jnp.float32)
    act = jax.nn.silu(pre).astype(jnp.bfloat16)
    return jnp.dot(act, down_proj, preferred_element_type=jnp.float32).astype(jnp.bfloat16)


def expert_backward(rows, grad_rows, up_proj, down_proj):
    pre = jnp.dot(rows, up_proj, preferred_element_type=jnp.float32)
    act = jax.nn.silu(pre).astype(jnp.bfloat16)
    dact = lax.dot_general(
        grad_rows, down_proj, (((1,), (1,)), ((), ())), preferred_element_type=jnp.float32
    )
    dpre = (dact * silu_grad(pre)).astype(jnp.bfloat16)
    dpart = lax.dot_general(
        dpre, up_proj, (((1,), (1,)), ((), ())), preferred_element_type=jnp.float32
    ).astype(jnp.bfloat16)
    grad_up = lax.dot_general(
        rows, dpre, (((0,), (0,)), ((), ())), preferred_element_type=jnp.float32
    )
    grad_down = lax.dot_general(
        act, grad_rows, (((0,), (0,)), ((), ())), preferred_element_type=jnp.float32
    )
    return (dpart, grad_up, grad_down)


def local(
    fwd_acts, fwd_routes, fwd_gates, back_acts, back_routes, back_gates, back_grads, w_up, w_down
):
    devices = lax.axis_size("expert")
    experts = devices // GROUP
    tok_rows = fwd_acts.shape[1]
    top_count = fwd_routes.shape[2]
    slot_cap = GROUP * (5 * tok_rows * top_count // (4 * devices))
    up_proj = w_up[0, 0]
    down_proj = w_down[0, 0]
    fwd_input = fwd_acts[0]
    back_input = back_acts[0]
    out_grad = back_grads[0]
    plain_f, gated_f = tables(fwd_routes[0], fwd_gates[0], experts, slot_cap)
    plain_b, gated_b = tables(back_routes[0], back_gates[0], experts, slot_cap)
    buffer_f = gather_rows(plain_f, fwd_input)
    buffer_x = gather_rows(plain_b, back_input)
    buffer_g = lax.dot_general(
        gated_b, out_grad.astype(jnp.float32), (((0,), (0,)), ((), ())), precision=HIGH
    ).astype(jnp.bfloat16)
    got_f = send_rows(buffer_f[None], experts, slot_cap)
    part = expert_forward(got_f[0], up_proj, down_proj)
    summed_f = send_back(part[None], experts, slot_cap)[0]
    got_b = send_rows(jnp.stack([buffer_x, buffer_g]), experts, slot_cap)
    dpart, grad_up, grad_down = expert_backward(got_b[0], got_b[1], up_proj, down_proj)
    summed_b = send_back(dpart[None], experts, slot_cap)[0]
    merged = jnp.dot(gated_f, summed_f, precision=HIGH)
    section_out = (fwd_input.astype(jnp.float32) + merged).astype(jnp.bfloat16)
    spread_back = jnp.dot(plain_b, summed_b, precision=HIGH)
    section_grad = (out_grad.astype(jnp.float32) + spread_back).astype(jnp.bfloat16)
    fwd_next = passed_along(section_out[None], "pipe", 1)
    back_next = passed_along(section_grad[None], "pipe", -1)
    return (fwd_next, back_next, grad_up[None, None], grad_down[None, None])


def solution(mesh):
    in_specs = (
        P("pipe", "expert", None),
        P("pipe", "expert", None),
        P("pipe", "expert", None),
        P("pipe", "expert", None),
        P("pipe", "expert", None),
        P("pipe", "expert", None),
        P("pipe", "expert", None),
        P("pipe", "expert", None, None),
        P("pipe", "expert", None, None),
    )
    out_specs = (
        P("pipe", "expert", None),
        P("pipe", "expert", None),
        P("pipe", "expert", None, None),
        P("pipe", "expert", None, None),
    )
    return jax.shard_map(local, mesh=mesh, in_specs=in_specs, out_specs=out_specs, check_vma=False)
```

profile of v0, /device:TPU:6, one launch (start us, length us, event | category | flops | bytes accessed | tf_op | source)
XLA Modules:
  0.0 673.3 jit_solution(2642117069289322087)
XLA Ops:
  0.6 0.9 copy.40
  1.8 0.2 reduce_window_sum.17
  2.0 0.2 select_reduce_fusion.3
  2.4 0.7 bitcast_add_fusion.1
  3.1 0.8 convert_reduce_fusion.3
  3.8 2.5 convolution_convert_fusion.4
  6.3 1.4 reshape_broadcast_in_dim.9
  7.7 2.9 broadcast_in_dim.26
  10.6 9.2 %all-to-all-start = ((bf16[1,32,20,3584]{3,2,0,1:T(8,128)(2,1)}), bf16[1,32,20,3584]{3,2,0,1:T(8,128)(2,1)}, u32[]{:S(2)}, u32[]{:S(2)}) async-start(bf16[1,32,20,3584]{3,2,0,1:T(8,128)(2,1)} %bitcast.71), calls=%async_computation | async-start | bytes 11010048 | tf_op jit(solution)/shard_map/all_to_all | solution.py:52
  20.1 0.2 reduce_window_sum.18
  20.8 1.5 convolution_convert_fusion.3
  22.3 1.4 stack.9
  23.7 3.1 convolution_convert_fusion.2
  26.8 2.3 stack.10
  29.1 1.7 maximum_bitcast_fusion
  30.7 3.7 copy.45
  34.5 108.8 %all-to-all-done = bf16[1,32,20,3584]{3,2,0,1:T(8,128)(2,1)} async-done(((bf16[1,32,20,3584]{3,2,0,1:T(8,128)(2,1)}), bf16[1,32,20,3584]{3,2,0,1:T(8,128)(2,1)}, u32[]{:S(2)}, u32[]{:S(2)}) %all-to-all-start) | async-done | bytes 4587552 | tf_op jit(solution)/shard_map/all_to_all | solution.py:52
  143.3 7.1 %broadcast_in_dim.29 = bf16[2,8,1,4,20,3584]{5,0,4,3,1,2:T(2,128)(2,1)} broadcast(bf16[2,8,20,3584]{3,0,2,1:T(2,128)(2,1)} %copy.45), dimensions={0,1,4,5} | broadcast | bytes 11468800 | tf_op jit(solution)/shard_map/broadcast_in_dim | solution.py:50
  150.4 5.0 all-to-all-start.2
  155.3 7.3 %squeeze_reshape.9 = bf16[640,3584]{1,0:T(8,128)(2,1)} reshape(bf16[1,32,20,3584]{3,2,0,1:T(8,128)(2,1)} %all-to-all-done) | data formatting | bytes 9175040 | tf_op jit(solution)/shard_map/squeeze;reshape | solution.py:112
  162.6 9.8 %convolution_convert_fusion.1 = bf16[640,3584]{1,0:T(8,128)(2,1)} fusion(bf16[1,1,256,3584]{3,2,1,0:T(8,128)(2,1)} %param.17, bf16[640,3584]{1,0:T(8,128)(2,1)} %squeeze_reshape.9, bf16[1,1,3584,256]{3,2,1,0:T(8,128)(2,1)S(1)} %copy-done), kind=kOutput, calls=%fused_computation.5 | convolution fusion | flops 2351923200 | bytes 12845056 | tf_op jit(solution)/shard_map/dot_general | solution.py:69
  172.5 7.2 %reshape_broadcast_in_dim.10 = bf16[1,32,20,3584]{3,2,1,0:T(8,128)(2,1)} reshape(bf16[640,3584]{1,0:T(8,128)(2,1)} %convolution_convert_fusion.1) | data formatting | bytes 9175040 | tf_op jit(solution)/shard_map/reshape;broadcast_in_dim | solution.py:58
  179.7 177.8 %all-to-all-done.2 = bf16[2,32,20,3584]{3,0,2,1:T(2,128)(2,1)} async-done(((bf16[2,32,20,3584]{3,0,2,1:T(2,128)(2,1)}), bf16[2,32,20,3584]{3,0,2,1:T(2,128)(2,1)}, u32[]{:S(2)}, u32[]{:S(2)}) %all-to-all-start.2) | async-done | bytes 9175072 | tf_op jit(solution)/shard_map/all_to_all | solution.py:52
  357.5 5.1 all-to-all-start.1
  362.6 45.7 %slice_reduce_fusion = (bf16[32,20,3584]{2,1,0:T(8,128)(2,1)}, bf16[32,20,3584]{2,1,0:T(8,128)(2,1)}) fusion(bf16[2,32,20,3584]{3,0,2,1:T(2,128)(2,1)} %all-to-all-done.2), kind=kLoop, calls=%fused_computation.2 | loop fusion | bytes 18350080 | tf_op jit(solution)/shard_map/slice | solution.py:115
  408.3 7.3 %squeeze.27 = bf16[640,3584]{1,0:T(8,128)(2,1)} reshape(bf16[32,20,3584]{2,1,0:T(8,128)(2,1)} %get-tuple-element.4) | data formatting | bytes 9175040 | tf_op jit(solution)/shard_map/squeeze | solution.py:115
  415.6 7.3 %squeeze.26 = bf16[640,3584]{1,0:T(8,128)(2,1)} reshape(bf16[32,20,3584]{2,1,0:T(8,128)(2,1)} %get-tuple-element.5) | data formatting | bytes 9175040 | tf_op jit(solution)/shard_map/squeeze | solution.py:115
  422.8 3.8 fusion.8
  426.6 0.5 copy-done.7
  427.1 1.4 fusion.15
  428.5 3.6 convolution_convert_fusion
  432.1 7.3 %reshape_broadcast_in_dim.11 = bf16[1,32,20,3584]{3,2,1,0:T(8,128)(2,1)} reshape(bf16[640,3584]{1,0:T(8,128)(2,1)} %convolution_convert_fusion) | data formatting | bytes 9175040 | tf_op jit(solution)/shard_map/reshape;broadcast_in_dim | solution.py:58
  439.3 46.5 %all-to-all-done.1 = bf16[1,32,20,3584]{3,2,0,1:T(8,128)(2,1)} async-done(((bf16[1,32,20,3584]{3,2,0,1:T(8,128)(2,1)}), bf16[1,32,20,3584]{3,2,0,1:T(8,128)(2,1)}, u32[]{:S(2)}, u32[]{:S(2)}) %all-to-all-start.1) | async-done | bytes 4587552 | tf_op jit(solution)/shard_map/all_to_all | solution.py:59
  485.9 4.9 all-to-all-start.3
  490.8 5.3 convert_reduce_fusion.1
  496.0 2.9 squeeze_reshape.10
  499.0 3.7 fusion.3
  502.7 4.5 collective-permute-start
  507.2 5.8 convolution_bitcast_fusion.1
  513.0 120.9 %all-to-all-done.3 = bf16[1,32,20,3584]{3,2,0,1:T(8,128)(2,1)} async-done(((bf16[1,32,20,3584]{3,2,0,1:T(8,128)(2,1)}), bf16[1,32,20,3584]{3,2,0,1:T(8,128)(2,1)}, u32[]{:S(2)}, u32[]{:S(2)}) %all-to-all-start.3) | async-done | bytes 4587552 | tf_op jit(solution)/shard_map/all_to_all | solution.py:59
  633.9 5.3 convert_reduce_fusion
  639.2 2.9 squeeze_reshape.11
  642.1 3.0 fusion.2
  645.1 4.8 collective-permute-start.1
  649.9 5.8 convolution_bitcast_fusion
  655.7 15.0 %collective-permute-done.1 = bf16[1,64,3584]{2,1,0:T(8,128)(2,1)S(1)} collective-permute-done((bf16[1,64,3584]{2,1,0:T(8,128)(2,1)S(1)}, bf16[1,64,3584]{2,1,0:T(8,128)(2,1)S(1)}, u32[]{:S(2)}, u32[]{:S(2)}) %collective-permute-start.1) | collective-permute-done | bytes 458784 | tf_op jit(solution)/shard_map/ppermute | solution.py:13
  670.7 1.8 copy.51
  672.5 0.8 copy.52
  (28 shorter events, 1.3 us)
Async XLA Ops:
  0.6 162.0 %copy-start = (bf16[1,1,3584,256]{3,2,1,0:T(8,128)(2,1)S(1)}, bf16[1,1,3584,256]{3,2,1,0:T(8,128)(2,1)}, u32[]{:S(2)}) copy-start(bf16[1,1,3584,256]{3,2,1,0:T(8,128)(2,1)} %param.16) | copy-start | bytes 5505028
  10.6 9.2 %copy-start.5 = (s32[1,64,2]{1,2,0:T(2,128)S(1)}, s32[1,64,2]{1,2,0:T(2,128)}, u32[]{:S(2)}) copy-start(s32[1,64,2]{1,2,0:T(2,128)} %param.13) | copy-start | bytes 1540
  10.6 10.1 %copy-start.6 = (f32[1,64,2]{1,2,0:T(2,128)S(1)}, f32[1,64,2]{1,2,0:T(2,128)}, u32[]{:S(2)}) copy-start(f32[1,64,2]{1,2,0:T(2,128)} %param.14) | copy-start | bytes 1540
  10.6 10.2 %copy-start.4 = (bf16[1,64,3584]{2,1,0:T(8,128)(2,1)S(1)}, bf16[1,64,3584]{2,1,0:T(8,128)(2,1)}, u32[]{:S(2)}) copy-start(bf16[1,64,3584]{2,1,0:T(8,128)(2,1)} %param.12) | copy-start | bytes 1376260
  10.6 132.7 %all-to-all-start = ((bf16[1,32,20,3584]{3,2,0,1:T(8,128)(2,1)}), bf16[1,32,20,3584]{3,2,0,1:T(8,128)(2,1)}, u32[]{:S(2)}, u32[]{:S(2)}) async-start(bf16[1,32,20,3584]{3,2,0,1:T(8,128)(2,1)} %bitcast.71), calls=%async_computation | async-start | bytes 11010048 | tf_op jit(solution)/shard_map/all_to_all | solution.py:52
  150.4 207.1 %all-to-all-start.2 = ((bf16[2,32,20,3584]{3,0,2,1:T(2,128)(2,1)}), bf16[2,32,20,3584]{3,0,2,1:T(2,128)(2,1)}, u32[]{:S(2)}, u32[]{:S(2)}) async-start(bf16[2,32,20,3584]{3,0,2,1:T(2,128)(2,1)} %bitcast.70), calls=%async_computation.2 | async-start | bytes 18350080 | tf_op jit(solution)/shard_map/all_to_all | solution.py:52
  357.5 128.4 %all-to-all-start.1 = ((bf16[1,32,20,3584]{3,2,0,1:T(8,128)(2,1)}), bf16[1,32,20,3584]{3,2,0,1:T(8,128)(2,1)}, u32[]{:S(2)}, u32[]{:S(2)}) async-start(bf16[1,32,20,3584]{3,2,0,1:T(8,128)(2,1)} %bitcast.73), calls=%async_computation.1 | async-start | bytes 11010048 | tf_op jit(solution)/shard_map/all_to_all | solution.py:59
  422.8 3.8 copy-start.1
  422.8 4.3 copy-start.7
  485.9 148.0 %all-to-all-start.3 = ((bf16[1,32,20,3584]{3,2,0,1:T(8,128)(2,1)}), bf16[1,32,20,3584]{3,2,0,1:T(8,128)(2,1)}, u32[]{:S(2)}, u32[]{:S(2)}) async-start(bf16[1,32,20,3584]{3,2,0,1:T(8,128)(2,1)} %bitcast.72), calls=%async_computation.3 | async-start | bytes 11010048 | tf_op jit(solution)/shard_map/all_to_all | solution.py:59
  496.0 2.9 copy-start.2
  502.7 153.0 %collective-permute-start = (bf16[1,64,3584]{2,1,0:T(8,128)(2,1)}, bf16[1,64,3584]{2,1,0:T(8,128)(2,1)}, u32[]{:S(2)}, u32[]{:S(2)}) collective-permute-start(bf16[1,64,3584]{2,1,0:T(8,128)(2,1)} %fusion.3), channel_id=1, source_target_pairs={{0,32},{32,64},{64,96},{96,128},{128,160},{160,192},{192,224},{224... | collective-permute-start | bytes 1376264 | tf_op jit(solution)/shard_map/ppermute | solution.py:13
  639.2 2.9 copy-start.3
  645.1 25.6 %collective-permute-start.1 = (bf16[1,64,3584]{2,1,0:T(8,128)(2,1)S(1)}, bf16[1,64,3584]{2,1,0:T(8,128)(2,1)S(1)}, u32[]{:S(2)}, u32[]{:S(2)}) collective-permute-start(bf16[1,64,3584]{2,1,0:T(8,128)(2,1)S(1)} %fusion.2), channel_id=1, source_target_pairs={{0,224},{32,0},{64,32},{96,64},{128,96},{160,128},{192,160},{224,1... | collective-permute-start | bytes 1376264 | tf_op jit(solution)/shard_map/ppermute | solution.py:13
where the time goes:
time: 675 us; the launch traced here: 673 us
  waiting for transfers between devices  469 us (69%)
  local copies, waits for them, and re-layouts  111 us (16%)
  matrix products  43.9 us (7%)
  starting transfers between devices  33.4 us (5%)
  other arithmetic  14.7 us (2%)
    all_to_all x2, waiting for transfers between devices, send_rows(): lax.all_to_all(copies, 'expert', split_axis=1, concat_axis=1, tiled=True)  287 us
    all_to_all x2, waiting for transfers between devices, send_back(): lax.all_to_all(arranged, 'expert', split_axis=1, concat_axis=1, tiled=True)  167 us
    slice x1, local copies, waits for them, and re-layouts, local(): got_b[0]  45.7 us
    ppermute x2, waiting for transfers between devices, passed_along(): return lax.ppermute(value, axis, pairs)  15 us
    another operation x2, local copies, waits for them, and re-layouts, send_back(): arranged = parts.reshape(count, experts * GROUP, slot_cap, model_width)  14.5 us
    all_to_all x2, starting transfers between devices, send_rows(): lax.all_to_all(copies, 'expert', split_axis=1, concat_axis=1, tiled=True)  14.2 us
  transfers between devices with their start and end apart: 6, of which 5 were waited for; matrix products, arithmetic and copies ran while one was open for 22% of the time, Pallas kernels for 0%

commit v1 on v0

--- a/solution.py
+++ b/solution.py
@@ -49,7 +49,9 @@
     count, _, model_width = stacked.shape
     copies = jnp.repeat(stacked.reshape(count, experts, 1, slot_cap, model_width), GROUP, axis=2)
     copies = copies.reshape(count, experts * GROUP, slot_cap, model_width)
-    received = lax.all_to_all(copies, "expert", split_axis=1, concat_axis=1, tiled=True)
+    pieces = jnp.split(copies, lax.axis_size("expert"), axis=1)
+    incoming = lax.all_to_all(jnp.stack(pieces), "expert", 0, 0)
+    received = jnp.concatenate(incoming, axis=1)
     return received.reshape(count, -1, model_width)
 
 

time: 675 us -> 693 us (1.027)
  local copies, waits for them, and re-layouts: 111 us -> 157 us
  waiting for transfers between devices: 469 us -> 436 us
    unnamed x20 -> x82, local copies, waits for them, and re-layouts: 4.07 us -> 53.5 us
    all_to_all x2, waiting for transfers between devices: 287 us -> 253 us  [send_rows(): incoming = lax.all_to_all(jnp.stack(pieces), 'expert', 0, 0)]
  transfers between devices with their start and end apart: 6 -> 6, of which waited for: 5 -> 5; matrix products, arithmetic and copies ran while one was open for 22% -> 27% of each run, Pallas kernels for 0% -> 0%
where the time goes in v1:
time: 693 us; the launch traced here: 686 us
  waiting for transfers between devices  436 us (63%)
  local copies, waits for them, and re-layouts  157 us (23%)
  matrix products  44 us (6%)
  starting transfers between devices  33.6 us (5%)
  other arithmetic  14.7 us (2%)
    all_to_all x2, waiting for transfers between devices, send_rows(): incoming = lax.all_to_all(jnp.stack(pieces), 'expert', 0, 0)  253 us
    all_to_all x2, waiting for transfers between devices, send_back(): lax.all_to_all(arranged, 'expert', split_axis=1, concat_axis=1, tiled=True)  168 us
    unnamed x82, local copies, waits for them, and re-layouts  53.5 us
    slice x1, local copies, waits for them, and re-layouts, local(): got_b[0]  45.5 us
    ppermute x2, waiting for transfers between devices, passed_along(): return lax.ppermute(value, axis, pairs)  15 us
    another operation x2, local copies, waits for them, and re-layouts, send_back(): arranged = parts.reshape(count, experts * GROUP, slot_cap, model_width)  14.4 us
    all_to_all x2, starting transfers between devices, send_rows(): incoming = lax.all_to_all(jnp.stack(pieces), 'expert', 0, 0)  14.1 us
  transfers between devices with their start and end apart: 6, of which 5 were waited for; matrix products, arithmetic and copies ran while one was open for 27% of the time, Pallas kernels for 0%

profile of v1, /device:TPU:6, one launch (start us, length us, event | category | flops | bytes accessed | tf_op | source)
XLA Modules:
  0.0 685.9 jit_solution(16961208745814352707)
XLA Ops:
  3.8 2.5 convolution_convert_fusion.4
  6.3 1.4 reshape_broadcast_in_dim.9
  29.9 9.2 %all-to-all-start = ((bf16[32,1,1,20,3584]{4,3,2,1,0:T(8,128)(2,1)}), bf16[32,1,1,20,3584]{4,3,2,1,0:T(8,128)(2,1)}, u32[]{:S(2)}, u32[]{:S(2)}) async-start(bf16[32,1,1,20,3584]{4,3,2,1,0:T(8,128)(2,1)} %fusion.59), calls=%async_computation | async-start | bytes 11010048 | tf_op jit(solution)/shard_map/all_to_all | solution.py:53
  40.2 1.5 convolution_convert_fusion.3
  41.6 1.4 stack.240
  43.0 3.1 convolution_convert_fusion.2
  46.1 2.3 stack.241
  48.4 1.7 maximum_bitcast_fusion
  50.1 2.4 copy.139
  52.4 5.6 broadcast_in_dim.29
  58.1 0.9 fusion.58
  69.0 0.9 fusion.46
  69.9 0.9 fusion.45
  70.8 1.0 fusion.44
  71.8 0.9 fusion.43
  73.6 0.9 fusion.41
  76.3 0.9 fusion.38
  81.8 0.9 fusion.32
  86.4 0.9 fusion.27
  87.3 75.3 %all-to-all-done = bf16[32,1,1,20,3584]{4,3,2,1,0:T(8,128)(2,1)} async-done(((bf16[32,1,1,20,3584]{4,3,2,1,0:T(8,128)(2,1)}), bf16[32,1,1,20,3584]{4,3,2,1,0:T(8,128)(2,1)}, u32[]{:S(2)}, u32[]{:S(2)}) %all-to-all-start) | async-done | bytes 4587552 | tf_op jit(solution)/shard_map/all_to_all | solution.py:53
  162.6 5.0 all-to-all-start.2
  167.6 7.3 %squeeze_reshape_reshape.3 = bf16[640,3584]{1,0:T(8,128)(2,1)} reshape(bf16[32,1,1,20,3584]{4,3,2,1,0:T(8,128)(2,1)} %all-to-all-done) | data formatting | bytes 9175040 | tf_op jit(solution)/shard_map/squeeze;reshape;reshape | solution.py:114
  174.9 9.9 %convolution_convert_fusion.1 = bf16[640,3584]{1,0:T(8,128)(2,1)} fusion(bf16[1,1,256,3584]{3,2,1,0:T(8,128)(2,1)} %param.17, bf16[640,3584]{1,0:T(8,128)(2,1)} %squeeze_reshape_reshape.3, bf16[1,1,3584,256]{3,2,1,0:T(8,128)(2,1)S(1)} %copy-done), kind=kOutput, calls=%fused_computation.5 | convolution fusion | flops 2351923200 | bytes 12845056 | tf_op jit(solution)/shard_map/dot_general | solution.py:71
  184.8 7.2 %reshape_broadcast_in_dim.10 = bf16[1,32,20,3584]{3,2,1,0:T(8,128)(2,1)} reshape(bf16[640,3584]{1,0:T(8,128)(2,1)} %convolution_convert_fusion.1) | data formatting | bytes 9175040 | tf_op jit(solution)/shard_map/reshape;broadcast_in_dim | solution.py:60
  192.0 177.8 %all-to-all-done.2 = bf16[32,2,1,20,3584]{4,1,3,2,0:T(2,128)(2,1)} async-done(((bf16[32,2,1,20,3584]{4,1,3,2,0:T(2,128)(2,1)}), bf16[32,2,1,20,3584]{4,1,3,2,0:T(2,128)(2,1)}, u32[]{:S(2)}, u32[]{:S(2)}) %all-to-all-start.2) | async-done | bytes 9175072 | tf_op jit(solution)/shard_map/all_to_all | solution.py:53
  369.7 5.1 all-to-all-start.1
  374.8 45.5 %slice_reduce_fusion = (bf16[32,20,3584]{2,1,0:T(8,128)(2,1)}, bf16[32,20,3584]{2,1,0:T(8,128)(2,1)}) fusion(bf16[2,32,1,20,3584]{4,0,3,2,1:T(2,128)(2,1)} %bitcast.79), kind=kLoop, calls=%fused_computation.2 | loop fusion | bytes 18350080 | tf_op jit(solution)/shard_map/slice | solution.py:117
  420.2 7.3 %squeeze.27 = bf16[640,3584]{1,0:T(8,128)(2,1)} reshape(bf16[32,20,3584]{2,1,0:T(8,128)(2,1)} %get-tuple-element.4) | data formatting | bytes 9175040 | tf_op jit(solution)/shard_map/squeeze | solution.py:117
  427.5 7.3 %squeeze.26 = bf16[640,3584]{1,0:T(8,128)(2,1)} reshape(bf16[32,20,3584]{2,1,0:T(8,128)(2,1)} %get-tuple-element.5) | data formatting | bytes 9175040 | tf_op jit(solution)/shard_map/squeeze | solution.py:117
  434.8 3.8 fusion.8
  439.1 1.4 fusion.15
  440.5 3.6 convolution_convert_fusion
  444.1 7.2 %reshape_broadcast_in_dim.11 = bf16[1,32,20,3584]{3,2,1,0:T(8,128)(2,1)} reshape(bf16[640,3584]{1,0:T(8,128)(2,1)} %convolution_convert_fusion) | data formatting | bytes 9175040 | tf_op jit(solution)/shard_map/reshape;broadcast_in_dim | solution.py:60
  451.3 47.0 %all-to-all-done.1 = bf16[1,32,20,3584]{3,2,0,1:T(8,128)(2,1)} async-done(((bf16[1,32,20,3584]{3,2,0,1:T(8,128)(2,1)}), bf16[1,32,20,3584]{3,2,0,1:T(8,128)(2,1)}, u32[]{:S(2)}, u32[]{:S(2)}) %all-to-all-start.1) | async-done | bytes 4587552 | tf_op jit(solution)/shard_map/all_to_all | solution.py:61
  498.3 4.9 all-to-all-start.3
  503.2 5.3 convert_reduce_fusion.1
  508.4 2.9 squeeze_reshape.6
  511.3 3.7 fusion.3
  515.0 4.7 collective-permute-start
  519.8 5.8 convolution_bitcast_fusion.1
  525.6 120.7 %all-to-all-done.3 = bf16[1,32,20,3584]{3,2,0,1:T(8,128)(2,1)} async-done(((bf16[1,32,20,3584]{3,2,0,1:T(8,128)(2,1)}), bf16[1,32,20,3584]{3,2,0,1:T(8,128)(2,1)}, u32[]{:S(2)}, u32[]{:S(2)}) %all-to-all-start.3) | async-done | bytes 4587552 | tf_op jit(solution)/shard_map/all_to_all | solution.py:61
  646.3 5.3 convert_reduce_fusion
  651.6 2.9 squeeze_reshape.7
  654.5 3.0 fusion.2
  657.5 4.8 collective-permute-start.1
  662.3 5.8 convolution_bitcast_fusion
  668.0 15.0 %collective-permute-done.1 = bf16[1,64,3584]{2,1,0:T(8,128)(2,1)S(1)} collective-permute-done((bf16[1,64,3584]{2,1,0:T(8,128)(2,1)S(1)}, bf16[1,64,3584]{2,1,0:T(8,128)(2,1)S(1)}, u32[]{:S(2)}, u32[]{:S(2)}) %collective-permute-start.1) | collective-permute-done | bytes 458784 | tf_op jit(solution)/shard_map/ppermute | solution.py:13
  683.0 1.8 copy.207
  (92 shorter events, 48.5 us)
Async XLA Ops:
  0.6 174.3 %copy-start = (bf16[1,1,3584,256]{3,2,1,0:T(8,128)(2,1)S(1)}, bf16[1,1,3584,256]{3,2,1,0:T(8,128)(2,1)}, u32[]{:S(2)}) copy-start(bf16[1,1,3584,256]{3,2,1,0:T(8,128)(2,1)} %param.16) | copy-start | bytes 5505028
  29.9 9.2 %copy-start.5 = (s32[1,64,2]{1,2,0:T(2,128)S(1)}, s32[1,64,2]{1,2,0:T(2,128)}, u32[]{:S(2)}) copy-start(s32[1,64,2]{1,2,0:T(2,128)} %param.13) | copy-start | bytes 1540
  29.9 10.1 %copy-start.6 = (f32[1,64,2]{1,2,0:T(2,128)S(1)}, f32[1,64,2]{1,2,0:T(2,128)}, u32[]{:S(2)}) copy-start(f32[1,64,2]{1,2,0:T(2,128)} %param.14) | copy-start | bytes 1540
  29.9 10.2 %copy-start.4 = (bf16[1,64,3584]{2,1,0:T(8,128)(2,1)S(1)}, bf16[1,64,3584]{2,1,0:T(8,128)(2,1)}, u32[]{:S(2)}) copy-start(bf16[1,64,3584]{2,1,0:T(8,128)(2,1)} %param.12) | copy-start | bytes 1376260
  29.9 132.7 %all-to-all-start = ((bf16[32,1,1,20,3584]{4,3,2,1,0:T(8,128)(2,1)}), bf16[32,1,1,20,3584]{4,3,2,1,0:T(8,128)(2,1)}, u32[]{:S(2)}, u32[]{:S(2)}) async-start(bf16[32,1,1,20,3584]{4,3,2,1,0:T(8,128)(2,1)} %fusion.59), calls=%async_computation | async-start | bytes 11010048 | tf_op jit(solution)/shard_map/all_to_all | solution.py:53
  162.6 207.1 %all-to-all-start.2 = ((bf16[32,2,1,20,3584]{4,1,3,2,0:T(2,128)(2,1)}), bf16[32,2,1,20,3584]{4,1,3,2,0:T(2,128)(2,1)}, u32[]{:S(2)}, u32[]{:S(2)}) async-start(bf16[32,2,1,20,3584]{4,1,3,2,0:T(2,128)(2,1)} %fusion.27), calls=%async_computation.2 | async-start | bytes 18350080 | tf_op jit(solution)/shard_map/all_to_all | solution.py:53
  369.7 128.5 %all-to-all-start.1 = ((bf16[1,32,20,3584]{3,2,0,1:T(8,128)(2,1)}), bf16[1,32,20,3584]{3,2,0,1:T(8,128)(2,1)}, u32[]{:S(2)}, u32[]{:S(2)}) async-start(bf16[1,32,20,3584]{3,2,0,1:T(8,128)(2,1)} %bitcast.390), calls=%async_computation.1 | async-start | bytes 11010048 | tf_op jit(solution)/shard_map/all_to_all | solution.py:61
  434.8 3.8 copy-start.1
  434.8 4.3 copy-start.7
  498.3 148.0 %all-to-all-start.3 = ((bf16[1,32,20,3584]{3,2,0,1:T(8,128)(2,1)}), bf16[1,32,20,3584]{3,2,0,1:T(8,128)(2,1)}, u32[]{:S(2)}, u32[]{:S(2)}) async-start(bf16[1,32,20,3584]{3,2,0,1:T(8,128)(2,1)} %bitcast.389), calls=%async_computation.3 | async-start | bytes 11010048 | tf_op jit(solution)/shard_map/all_to_all | solution.py:61
  503.1 8.2 %copy-start.2 = (bf16[1,64,3584]{2,1,0:T(8,128)(2,1)S(1)}, bf16[1,64,3584]{2,1,0:T(8,128)(2,1)}, u32[]{:S(2)}) copy-start(bf16[1,64,3584]{2,1,0:T(8,128)(2,1)} %param.9) | copy-start | bytes 1376260
  515.0 153.0 %collective-permute-start = (bf16[1,64,3584]{2,1,0:T(8,128)(2,1)}, bf16[1,64,3584]{2,1,0:T(8,128)(2,1)}, u32[]{:S(2)}, u32[]{:S(2)}) collective-permute-start(bf16[1,64,3584]{2,1,0:T(8,128)(2,1)} %fusion.3), channel_id=1, source_target_pairs={{0,32},{32,64},{64,96},{96,128},{128,160},{160,192},{192,224},{224... | collective-permute-start | bytes 1376264 | tf_op jit(solution)/shard_map/ppermute | solution.py:13
  646.3 8.2 %copy-start.3 = (bf16[1,64,3584]{2,1,0:T(8,128)(2,1)S(1)}, bf16[1,64,3584]{2,1,0:T(8,128)(2,1)}, u32[]{:S(2)}) copy-start(bf16[1,64,3584]{2,1,0:T(8,128)(2,1)} %param.15) | copy-start | bytes 1376260
  657.5 25.6 %collective-permute-start.1 = (bf16[1,64,3584]{2,1,0:T(8,128)(2,1)S(1)}, bf16[1,64,3584]{2,1,0:T(8,128)(2,1)S(1)}, u32[]{:S(2)}, u32[]{:S(2)}) collective-permute-start(bf16[1,64,3584]{2,1,0:T(8,128)(2,1)S(1)} %fusion.2), channel_id=1, source_target_pairs={{0,224},{32,0},{64,32},{96,64},{128,96},{160,128},{192,160},{224,1... | collective-permute-start | bytes 1376264 | tf_op jit(solution)/shard_map/ppermute | solution.py:13
